TPU v7x, 32 devices: a whole 2x2x4 slice. The times are simulated.
32 devices in a mesh: blk: 8 (over z, y), grp: 4 (over x, core).
Axes of the slice: x: 2, y: 2, z: 4, core: 2. Of those that a mesh axis runs over, the one named last changes fastest.
Arguments:
- tables: float32 [8, 8192, 128], P('grp', 'blk'), may hold values from -1 to 1
- bag_ids: int32 [1024, 8, 32], P('blk', 'grp'), may hold values from 0 to 8191, as said below
Outputs:
- pooled: float32 [1024, 8, 128], P('blk', 'grp')
- interaction: float32 [1024, 8, 8], P('blk', 'grp')
Inputs may be any that keep to these rules, and one draw needn't show every extreme that they name: `bag_ids`: some rows are far more popular than others.
All inputs are finite; a program needn't handle non-finite values.
Results may differ from a plain program's by a relative error of at most 0.000065.
Values sent between devices are 32-bit elements; how exact they have to be, the bound alone decides.
A program may use at most 64 MiB of HBM per device.

v0:
```python
import jax
import jax.numpy as jnp
from jax import lax
from jax.sharding import PartitionSpec as P

SECTIONS = 8


def from_behind(value, axis, steps):
    count = lax.axis_size(axis)
    pairs = [(source, (source + steps) % count) for source in range(count)]
    return lax.ppermute(value, axis, pairs)


def pool_shard(table_rows, bag_codes, offset):
    samples = bag_codes.shape[0]
    shard_rows = table_rows.shape[1]
    inside = (bag_codes % SECTIONS == offset).astype(jnp.float32)
    local_row = bag_codes // SECTIONS
    sample_index = jnp.arange(samples, dtype=jnp.int32)[:, None]
    results = []
    for table_num in range(table_rows.shape[0]):
        counts = jnp.zeros((samples, shard_rows), jnp.float32)
        counts = counts.at[sample_index, local_row[:, table_num, :]].add(inside[:, table_num, :])
        results.append(
            jnp.dot(
                counts,
                table_rows[table_num],
                precision=lax.Precision.HIGHEST,
                preferred_element_type=jnp.float32,
            )
        )
    return jnp.stack(results, axis=1)


def shards(tables, bag_ids):
    pooled = pool_shard(tables, bag_ids, 0)
    for offset in range(1, SECTIONS):
        arrived = from_behind(bag_ids, "blk", -offset)
        partial_value = pool_shard(tables, arrived, offset)
        pooled = pooled + from_behind(partial_value, "blk", offset)
    gathered = lax.all_gather(pooled, "grp", axis=1, tiled=True)
    interaction = (
        jnp.einsum("bte,bue->btu", pooled, gathered, precision=lax.Precision.HIGHEST)
        / pooled.shape[2]
    )
    return (pooled, interaction)


def solution(mesh):
    return jax.shard_map(
        shards,
        mesh=mesh,
        in_specs=(P("grp", "blk", None), P("blk", "grp", None)),
        out_specs=(P("blk", "grp", None), P("blk", "grp", None)),
        check_vma=False,
    )
```

profile of v0, /device:TPU:0, one launch (start us, length us, event | category | flops | bytes accessed | tf_op | source)
XLA Modules:
  0.0 522.3 jit_solution(8769694989029801037)
XLA Ops:
  0.6 5.1 collective-permute-start.4
  11.4 1.8 collective-permute-start.12
  15.4 3.0 collective-permute-done.12
  26.6 28.4 %scatter_custom_fusion = f32[131072]{0:T(1024)S(1)} fusion(s32[4096]{0:T(1024)S(1)} %reshape.518, f32[4096]{0:T(1024)S(1)} %reshape.520, f32[]{:T(128)} %constant.122.clone.1), kind=kCustom, calls=%fused_computation.96 | custom fusion | flops 4096 | bytes 524292
  55.2 28.4 %scatter_custom_fusion.2 = f32[131072]{0:T(1024)S(1)} fusion(s32[4096]{0:T(1024)S(1)} %reshape.530, f32[4096]{0:T(1024)S(1)} %reshape.532, f32[]{:T(128)} %constant.122.clone.1), kind=kCustom, calls=%fused_computation.92 | custom fusion | flops 4096 | bytes 524292
  85.0 28.4 %scatter_custom_fusion.4 = f32[131072]{0:T(1024)S(1)} fusion(s32[4096]{0:T(1024)S(1)} %reshape.542, f32[4096]{0:T(1024)S(1)} %reshape.544, f32[]{:T(128)} %constant.122.clone.1), kind=kCustom, calls=%fused_computation.88 | custom fusion | flops 4096 | bytes 524292
  114.2 28.6 %scatter_custom_fusion.6 = f32[131072]{0:T(1024)S(1)} fusion(s32[4096]{0:T(1024)S(1)} %reshape.554, f32[4096]{0:T(1024)S(1)} %reshape.556, f32[]{:T(128)} %constant.122.clone.1), kind=kCustom, calls=%fused_computation.84 | custom fusion | flops 4096 | bytes 524292
  143.5 28.4 %scatter_custom_fusion.8 = f32[131072]{0:T(1024)S(1)} fusion(s32[4096]{0:T(1024)S(1)} %reshape.566, f32[4096]{0:T(1024)S(1)} %reshape.568, f32[]{:T(128)} %constant.122.clone.1), kind=kCustom, calls=%fused_computation.80 | custom fusion | flops 4096 | bytes 524292
  172.7 28.4 %scatter_custom_fusion.14 = f32[131072]{0:T(1024)S(1)} fusion(s32[4096]{0:T(1024)S(1)} %reshape.602, f32[4096]{0:T(1024)S(1)} %reshape.604, f32[]{:T(128)} %constant.122.clone.1), kind=kCustom, calls=%fused_computation.68 | custom fusion | flops 4096 | bytes 524292
  201.8 28.4 %scatter_custom_fusion.12 = f32[131072]{0:T(1024)S(1)} fusion(s32[4096]{0:T(1024)S(1)} %reshape.590, f32[4096]{0:T(1024)S(1)} %reshape.592, f32[]{:T(128)} %constant.122.clone.1), kind=kCustom, calls=%fused_computation.72 | custom fusion | flops 4096 | bytes 524292
  231.0 28.4 %scatter_custom_fusion.10 = f32[131072]{0:T(1024)S(1)} fusion(s32[4096]{0:T(1024)S(1)} %reshape.578, f32[4096]{0:T(1024)S(1)} %reshape.580, f32[]{:T(128)} %constant.122.clone.1), kind=kCustom, calls=%fused_computation.76 | custom fusion | flops 4096 | bytes 524292
  260.2 28.4 %scatter_custom_fusion.3 = f32[131072]{0:T(1024)S(1)} fusion(s32[4096]{0:T(1024)S(1)} %reshape.536, f32[4096]{0:T(1024)S(1)} %reshape.538, f32[]{:T(128)} %constant.122.clone.1), kind=kCustom, calls=%fused_computation.90 | custom fusion | flops 4096 | bytes 524292
  289.4 2.5 collective-permute-start.1
  291.8 28.6 %scatter_custom_fusion.5 = f32[131072]{0:T(1024)S(1)} fusion(s32[4096]{0:T(1024)S(1)} %reshape.548, f32[4096]{0:T(1024)S(1)} %reshape.550, f32[]{:T(128)} %constant.122.clone.1), kind=kCustom, calls=%fused_computation.86 | custom fusion | flops 4096 | bytes 524292
  321.3 28.4 %scatter_custom_fusion.7 = f32[131072]{0:T(1024)S(1)} fusion(s32[4096]{0:T(1024)S(1)} %reshape.560, f32[4096]{0:T(1024)S(1)} %reshape.562, f32[]{:T(128)} %constant.122.clone.1), kind=kCustom, calls=%fused_computation.82 | custom fusion | flops 4096 | bytes 524292
  350.5 28.4 %scatter_custom_fusion.9 = f32[131072]{0:T(1024)S(1)} fusion(s32[4096]{0:T(1024)S(1)} %reshape.572, f32[4096]{0:T(1024)S(1)} %reshape.574, f32[]{:T(128)} %constant.122.clone.1), kind=kCustom, calls=%fused_computation.78 | custom fusion | flops 4096 | bytes 524292
  380.3 3.8 collective-permute-start.7
  384.2 28.4 %scatter_custom_fusion.15 = f32[131072]{0:T(1024)S(1)} fusion(s32[4096]{0:T(1024)S(1)} %reshape.608, f32[4096]{0:T(1024)S(1)} %reshape.610, f32[]{:T(128)} %constant.122.clone.1), kind=kCustom, calls=%fused_computation.66 | custom fusion | flops 4096 | bytes 524292
  414.0 3.8 collective-permute-start.13
  417.8 28.6 %scatter_custom_fusion.13 = f32[131072]{0:T(1024)S(1)} fusion(s32[4096]{0:T(1024)} %reshape.596, f32[4096]{0:T(1024)S(1)} %reshape.598, f32[]{:T(128)} %constant.122.clone.1), kind=kCustom, calls=%fused_computation.70 | custom fusion | flops 4096 | bytes 524800
  447.1 28.7 %scatter_custom_fusion.11 = f32[131072]{0:T(1024)S(1)} fusion(s32[4096]{0:T(1024)S(1)} %reshape.584, f32[4096]{0:T(1024)S(1)} %reshape.586, f32[]{:T(128)} %constant.122.clone.1), kind=kCustom, calls=%fused_computation.74 | custom fusion | flops 4096 | bytes 524292
  477.4 28.4 %scatter_custom_fusion.1 = f32[131072]{0:T(1024)S(1)} fusion(s32[4096]{0:T(1024)S(1)} %reshape.524, f32[4096]{0:T(1024)S(1)} %reshape.526, f32[]{:T(128)} %constant.122.clone.1), kind=kCustom, calls=%fused_computation.94 | custom fusion | flops 4096 | bytes 524292
  507.5 4.3 collective-permute-done.11
  512.8 7.2 %all_gather.3 = f32[128,8,128]{2,0,1:T(8,128)S(1)} all-gather(f32[128,2,128]{2,0,1:T(8,128)S(1)} %fusion.70), channel_id=1, replica_groups=mesh['blk'=8,'grp'=4] {'grp'}, dimensions={1}, use_global_device_ids=true | all-gather | bytes 655360 | tf_op jit(solution)/shard_map/all_gather | solution.py:42
  (183 shorter events, 33.3 us)
Async XLA Ops:
  0.6 10.3 %copy-start.3 = (s32[128,2,32]{0,2,1:T(8,128)S(1)}, s32[128,2,32]{0,2,1:T(8,128)}, u32[]{:S(2)}) copy-start(s32[128,2,32]{0,2,1:T(8,128)} %param.3) | copy-start | bytes 98308
  0.6 10.8 %collective-permute-start.4 = (s32[128,2,32]{0,2,1:T(8,128)}, s32[128,2,32]{0,2,1:T(8,128)S(1)}, u32[]{:S(2)}, u32[]{:S(2)}) collective-permute-start(s32[128,2,32]{0,2,1:T(8,128)} %param.3), channel_id=1, source_target_pairs={{0,20},{4,24},{8,28},{12,0},{16,4},{20,8},{24,12},{28,16},{1,21},{... | collective-permute-start | bytes 98312 | tf_op jit(solution)/shard_map/ppermute | solution.py:12
  5.7 7.6 %collective-permute-start.2 = (s32[128,2,32]{0,2,1:T(8,128)}, s32[128,2,32]{0,2,1:T(8,128)S(1)}, u32[]{:S(2)}, u32[]{:S(2)}) collective-permute-start(s32[128,2,32]{0,2,1:T(8,128)} %param.3), channel_id=1, source_target_pairs={{0,24},{4,28},{8,0},{12,4},{16,8},{20,12},{24,16},{28,20},{1,25},{... | collective-permute-start | bytes 98312 | tf_op jit(solution)/shard_map/ppermute | solution.py:12
  7.1 8.0 %collective-permute-start = (s32[128,2,32]{0,2,1:T(8,128)}, s32[128,2,32]{0,2,1:T(8,128)S(1)}, u32[]{:S(2)}, u32[]{:S(2)}) collective-permute-start(s32[128,2,32]{0,2,1:T(8,128)} %param.3), channel_id=1, source_target_pairs={{0,28},{4,0},{8,4},{12,8},{16,12},{20,16},{24,20},{28,24},{1,29},{... | collective-permute-start | bytes 98312 | tf_op jit(solution)/shard_map/ppermute | solution.py:12
  7.6 7.6 %collective-permute-start.8 = (s32[128,2,32]{0,2,1:T(8,128)}, s32[128,2,32]{0,2,1:T(8,128)S(1)}, u32[]{:S(2)}, u32[]{:S(2)}) collective-permute-start(s32[128,2,32]{0,2,1:T(8,128)} %param.3), channel_id=1, source_target_pairs={{0,12},{4,16},{8,20},{12,24},{16,28},{20,0},{24,4},{28,8},{1,13},{... | collective-permute-start | bytes 98312 | tf_op jit(solution)/shard_map/ppermute | solution.py:12
  9.2 6.1 %collective-permute-start.6 = (s32[128,2,32]{0,2,1:T(8,128)}, s32[128,2,32]{0,2,1:T(8,128)S(1)}, u32[]{:S(2)}, u32[]{:S(2)}) collective-permute-start(s32[128,2,32]{0,2,1:T(8,128)} %param.3), channel_id=1, source_target_pairs={{0,16},{4,20},{8,24},{12,28},{16,0},{20,4},{24,8},{28,12},{1,17},{... | collective-permute-start | bytes 98312 | tf_op jit(solution)/shard_map/ppermute | solution.py:12
  11.4 6.9 %collective-permute-start.12 = (s32[128,2,32]{0,2,1:T(8,128)S(1)}, s32[128,2,32]{0,2,1:T(8,128)S(1)}, u32[]{:S(2)}, u32[]{:S(2)}) collective-permute-start(s32[128,2,32]{0,2,1:T(8,128)S(1)} %copy-done.3), channel_id=1, source_target_pairs={{0,4},{4,8},{8,12},{12,16},{16,20},{20,24},{24,28},{28,0},{1,5},{5... | collective-permute-start | bytes 98312 | tf_op jit(solution)/shard_map/ppermute | solution.py:12
  13.4 5.8 %collective-permute-start.10 = (s32[128,2,32]{0,2,1:T(8,128)S(1)}, s32[128,2,32]{0,2,1:T(8,128)S(1)}, u32[]{:S(2)}, u32[]{:S(2)}) collective-permute-start(s32[128,2,32]{0,2,1:T(8,128)S(1)} %copy-done.3), channel_id=1, source_target_pairs={{0,8},{4,12},{8,16},{12,20},{16,24},{20,28},{24,0},{28,4},{1,9},{5... | collective-permute-start | bytes 98312 | tf_op jit(solution)/shard_map/ppermute | solution.py:12
  21.8 0.7 copy-start.5
  22.4 0.7 copy-start.4
  55.2 28.5 %copy-start = (f32[2,1024,128]{2,1,0:T(8,128)S(1)}, f32[2,1024,128]{2,1,0:T(8,128)}, u32[]{:S(2)}) copy-start(f32[2,1024,128]{2,1,0:T(8,128)} %param.2) | copy-start | bytes 3145732
  289.4 216.6 %collective-permute-start.1 = (f32[128,2,128]{2,0,1:T(8,128)S(1)}, f32[128,2,128]{2,0,1:T(8,128)S(1)}, u32[]{:S(2)}, u32[]{:S(2)}) collective-permute-start(f32[128,2,128]{2,0,1:T(8,128)S(1)} %pad_maximum_fusion), channel_id=1, source_target_pairs={{0,4},{4,8},{8,12},{12,16},{16,20},{20,24},{24,28},{28,0},{1,5},{5... | collective-permute-start | bytes 393224 | tf_op jit(solution)/shard_map/ppermute | solution.py:12
  321.2 185.6 %collective-permute-start.3 = (f32[128,2,128]{2,0,1:T(8,128)S(1)}, f32[128,2,128]{2,0,1:T(8,128)S(1)}, u32[]{:S(2)}, u32[]{:S(2)}) collective-permute-start(f32[128,2,128]{2,0,1:T(8,128)S(1)} %pad_maximum_fusion.1), channel_id=1, source_target_pairs={{0,8},{4,12},{8,16},{12,20},{16,24},{20,28},{24,0},{28,4},{1,9},{5... | collective-permute-start | bytes 393224 | tf_op jit(solution)/shard_map/ppermute | solution.py:12
  350.5 157.0 %collective-permute-start.5 = (f32[128,2,128]{2,0,1:T(8,128)S(1)}, f32[128,2,128]{2,0,1:T(8,128)S(1)}, u32[]{:S(2)}, u32[]{:S(2)}) collective-permute-start(f32[128,2,128]{2,0,1:T(8,128)S(1)} %pad_maximum_fusion.2), channel_id=1, source_target_pairs={{0,12},{4,16},{8,20},{12,24},{16,28},{20,0},{24,4},{28,8},{1,13},{... | collective-permute-start | bytes 393224 | tf_op jit(solution)/shard_map/ppermute | solution.py:12
  380.3 127.1 %collective-permute-start.7 = (f32[128,2,128]{2,0,1:T(8,128)}, f32[128,2,128]{2,0,1:T(8,128)S(1)}, u32[]{:S(2)}, u32[]{:S(2)}) collective-permute-start(f32[128,2,128]{2,0,1:T(8,128)} %pad_maximum_fusion.3), channel_id=1, source_target_pairs={{0,16},{4,20},{8,24},{12,28},{16,0},{20,4},{24,8},{28,12},{1,17},{... | collective-permute-start | bytes 393224 | tf_op jit(solution)/shard_map/ppermute | solution.py:12
  414.0 93.5 %collective-permute-start.13 = (f32[128,2,128]{2,0,1:T(8,128)}, f32[128,2,128]{2,0,1:T(8,128)S(1)}, u32[]{:S(2)}, u32[]{:S(2)}) collective-permute-start(f32[128,2,128]{2,0,1:T(8,128)} %pad_maximum_fusion.6), channel_id=1, source_target_pairs={{0,28},{4,0},{8,4},{12,8},{16,12},{20,16},{24,20},{28,24},{1,29},{... | collective-permute-start | bytes 393224 | tf_op jit(solution)/shard_map/ppermute | solution.py:12
  505.9 0.9 copy-start.2
  506.8 5.0 collective-permute-start.11
  506.8 5.9 %collective-permute-start.9 = (f32[128,2,128]{2,0,1:T(8,128)S(1)}, f32[128,2,128]{2,0,1:T(8,128)S(1)}, u32[]{:S(2)}, u32[]{:S(2)}) collective-permute-start(f32[128,2,128]{2,0,1:T(8,128)S(1)} %pad_maximum_fusion.4), channel_id=1, source_target_pairs={{0,20},{4,24},{8,28},{12,0},{16,4},{20,8},{24,12},{28,16},{1,21},{... | collective-permute-start | bytes 393224 | tf_op jit(solution)/shard_map/ppermute | solution.py:12
  512.8 7.2 %copy-start.1 = (f32[128,2,128]{2,1,0:T(2,128)}, f32[128,2,128]{2,1,0:T(2,128)S(1)}, u32[]{:S(2)}) copy-start(f32[128,2,128]{2,1,0:T(2,128)S(1)} %copy.62) | copy-start | bytes 393220
where the time goes:
time: 530 us; the launch traced here: 522 us
  other arithmetic  459 us (87%)
  starting transfers between devices  23.2 us (4%)
  matrix products  11.4 us (2%)
  local copies, waits for them, and re-layouts  10.5 us (2%)
  waiting for transfers between devices  8.9 us (2%)
  blocking collectives  7.17 us (1%)
    unnamed x26, other arithmetic  456 us
    ppermute x14, starting transfers between devices, from_behind(): return lax.ppermute(value, axis, pairs)  23.2 us
  transfers between devices with their start and end apart: 14, of which 4 were waited for; matrix products, arithmetic and copies ran while one was open for 40% of the time, Pallas kernels for 0%

commit v1 on v0

v1 whole, which is shorter than its diff:
```python
import functools

import jax
import jax.numpy as jnp
from jax import lax
from jax.experimental import pallas as pl
from jax.experimental.pallas import tpu as pltpu
from jax.sharding import PartitionSpec as P

SECTIONS = 8
MESH = pl.DeviceIdType.MESH
VMEM = pl.BlockSpec(memory_space=pltpu.VMEM)
CHUNK = 256
FAR = 1 << 20


def gather_ids_kernel(n, ids_ref, out_ref, send_sem, recv_sem):
    me = lax.axis_index("blk")
    rows = ids_ref.shape[0]
    barrier = pltpu.get_barrier_semaphore()
    count = 0
    for d in range(1, SECTIONS):
        pl.semaphore_signal(barrier, inc=1, device_id={"blk": lax.rem(me + d, n)}, device_id_type=MESH)
        count += 1
        if n != SECTIONS:
            pl.semaphore_signal(barrier, inc=1, device_id={"blk": lax.rem(me + n - d, n)}, device_id_type=MESH)
            count += 1
    pl.semaphore_wait(barrier, count)
    copies = []
    for d in range(1, SECTIONS):
        copy = pltpu.make_async_remote_copy(
            src_ref=ids_ref,
            dst_ref=out_ref.at[pl.ds(d * rows, rows)],
            send_sem=send_sem.at[d - 1],
            recv_sem=recv_sem.at[d - 1],
            device_id={"blk": lax.rem(me + n - d, n)},
            device_id_type=MESH,
        )
        copy.start()
        copies.append(copy)
    out_ref[pl.ds(0, rows)] = ids_ref[...]
    for copy in copies:
        copy.wait()


def gather_ids(n, ids):
    rows, lanes = ids.shape
    return pl.pallas_call(
        functools.partial(gather_ids_kernel, n),
        out_shape=jax.ShapeDtypeStruct((SECTIONS * rows, lanes), jnp.int32),
        in_specs=[VMEM],
        out_specs=VMEM,
        scratch_shapes=[
            pltpu.SemaphoreType.DMA((SECTIONS - 1,)),
            pltpu.SemaphoreType.DMA((SECTIONS - 1,)),
        ],
        compiler_params=pltpu.CompilerParams(collective_id=0, has_side_effects=True),
        name="gather_ids",
    )(ids)


def bitonic_merge(x):
    half = len(x) // 2
    if half == 0:
        return x
    low = [jnp.minimum(x[i], x[i + half]) for i in range(half)]
    high = [jnp.maximum(x[i], x[i + half]) for i in range(half)]
    return bitonic_merge(low) + bitonic_merge(high)


def bitonic_sort(x):
    if len(x) == 1:
        return x
    half = len(x) // 2
    return bitonic_merge(bitonic_sort(x[:half]) + bitonic_sort(x[half:])[::-1])


def pool_kernel(bag, ids_ref, table_ref, part_ref, keys, counts, table_t):
    tables, rows, width = table_ref.shape
    groups = ids_ref.shape[0] // bag
    lanes = ids_ref.shape[1]
    chunks = rows // CHUNK
    for t in range(tables):
        whole = table_ref[t]
        flipped = whole.T
        high = flipped.astype(jnp.bfloat16)
        table_t[t, pl.ds(0, width), :] = high
        table_t[t, pl.ds(width, width), :] = (flipped - high.astype(jnp.float32)).astype(jnp.bfloat16)
    section = lax.broadcasted_iota(jnp.int32, (groups, lanes), 0) // tables
    entries = []
    for p in range(bag):
        code = ids_ref[pl.ds(p, groups, stride=bag), :]
        entries.append(jnp.where((code & (SECTIONS - 1)) == section, code >> 3, FAR))
    entries = bitonic_sort(entries)
    pairs = SECTIONS // 2
    trips = []
    for c in range(chunks):
        inside = [
            jnp.where((x >= c * CHUNK) & (x < (c + 1) * CHUNK), x - c * CHUNK, FAR) for x in entries
        ]
        inside = bitonic_merge(inside)
        used = jnp.zeros((groups, lanes), jnp.int32)
        for p in range(bag):
            used = used + (inside[p] < FAR).astype(jnp.int32)
            keys[c, p] = inside[p].astype(jnp.float32)
        step = groups // pairs
        trips.append([jnp.max(used[q * step : (q + 1) * step]) for q in range(pairs)])
    index = lax.broadcasted_iota(jnp.int32, (CHUNK, lanes), 0).astype(jnp.float32).astype(jnp.bfloat16)
    one, zero = jnp.bfloat16(1), jnp.bfloat16(0)
    for t in range(tables):
        for c in range(chunks):
            for q in range(pairs):
                places = [(2 * q) * tables + t, (2 * q + 1) * tables + t]

                def body(j, acc):
                    fresh = []
                    for place, total in zip(places, acc):
                        key = keys[c, j, pl.ds(place, 1), :]
                        key = jnp.broadcast_to(key, (CHUNK, lanes)).astype(jnp.bfloat16)
                        fresh.append(total + jnp.where(index == key, one, zero))
                    return tuple(fresh)

                empty = jnp.zeros((CHUNK, lanes), jnp.bfloat16)
                acc = lax.fori_loop(0, trips[c][q], body, (empty, empty))
                for i in range(2):
                    counts[pl.ds(c * CHUNK, CHUNK), pl.ds((2 * q + i) * lanes, lanes)] = acc[i]
        for q in range(pairs):
            total = jnp.dot(
                table_t[t], counts[:, pl.ds(2 * q * lanes, 2 * lanes)], preferred_element_type=jnp.float32
            )
            total = total[:width] + total[width:]
            for i in range(2):
                part_ref[2 * q + i, t] = total[:, i * lanes : (i + 1) * lanes]


def pool(bag, ids, tables):
    count, rows, width = tables.shape
    lanes = ids.shape[1]
    groups = ids.shape[0] // bag
    return pl.pallas_call(
        functools.partial(pool_kernel, bag),
        out_shape=jax.ShapeDtypeStruct((SECTIONS, count, width, lanes), jnp.float32),
        in_specs=[VMEM, VMEM],
        out_specs=VMEM,
        scratch_shapes=[
            pltpu.VMEM((rows // CHUNK, bag, groups, lanes), jnp.float32),
            pltpu.VMEM((rows, SECTIONS * lanes), jnp.bfloat16),
            pltpu.VMEM((count, 2 * width, rows), jnp.bfloat16),
        ],
        name="pool",
    )(ids, tables)


PIECES = 2


def finish_kernel(n, groups, part_ref, pooled_ref, inter_ref, held, mixed, gram, grams, *sems):
    ring_send, ring_recv, mix_send, mix_recv, gram_send, gram_recv = sems
    sections, tables, width, lanes = part_ref.shape
    me, grp = lax.axis_index("blk"), lax.axis_index("grp")
    last = sections - 1
    piece = width // PIECES
    quarter = width // groups
    whole_ring = n == sections

    if whole_ring:
        place = jnp.where(me % 2 == 0, me // 2, n - 1 - me // 2)
        ways = [1 if t % 2 == 0 else n - 1 for t in range(tables)]
    else:
        place = me
        ways = [1 for t in range(tables)]

    def at(position):
        position = lax.rem(position, n)
        if whole_ring:
            return jnp.where(position < n // 2, 2 * position, 2 * (n - 1 - position) + 1)
        return position

    def section_of(t, away):
        return lax.rem(at(place + ways[t] * away) + n - me, n)

    barrier = pltpu.get_barrier_semaphore()
    for neighbour in (at(place + 1), at(place + n - 1)):
        pl.semaphore_signal(barrier, inc=1, device_id={"blk": neighbour}, device_id_type=MESH)
    for k in range(1, groups):
        pl.semaphore_signal(barrier, inc=1, device_id={"grp": lax.rem(grp + k, groups)}, device_id_type=MESH)
    pl.semaphore_wait(barrier, 2 + groups - 1)

    def hop(step, t, c, source):
        return pltpu.make_async_remote_copy(
            src_ref=source,
            dst_ref=held.at[step, t, pl.ds(c * piece, piece)],
            send_sem=ring_send.at[step, t, c],
            recv_sem=ring_recv.at[step, t, c],
            device_id={"blk": at(place + ways[t])},
            device_id_type=MESH,
        )

    flying = {}
    for c in range(PIECES):
        for t in range(tables):
            flying[0, t, c] = hop(0, t, c, part_ref.at[section_of(t, last), t, pl.ds(c * piece, piece)])
            flying[0, t, c].start()
    for step in range(last):
        for c in range(PIECES):
            for t in range(tables):
                rows = pl.ds(c * piece, piece)
                flying[step, t, c].wait_recv()
                total = held[step, t, rows] + part_ref[section_of(t, last - 1 - step), t, rows]
                if step + 1 < last:
                    held[step, t, rows] = total
                    flying[step + 1, t, c] = hop(step + 1, t, c, held.at[step, t, rows])
                    flying[step + 1, t, c].start()
                else:
                    pooled_ref[t, rows] = total

    mixes = []
    for k in range(1, groups):
        peer = lax.rem(grp + k, groups)
        mixes.append(
            pltpu.make_async_remote_copy(
                src_ref=pooled_ref.at[:, pl.ds(pl.multiple_of(peer * quarter, quarter), quarter)],
                dst_ref=mixed.at[grp],
                send_sem=mix_send.at[k - 1],
                recv_sem=mix_recv.at[k - 1],
                device_id={"grp": peer},
                device_id_type=MESH,
            )
        )
        mixes[-1].start()
    mixed[grp] = pooled_ref[:, pl.ds(pl.multiple_of(grp * quarter, quarter), quarter)]
    for copy in flying.values():
        copy.wait_send()
    for copy in mixes:
        copy.wait_recv()
    every = [mixed[g, t] for g in range(groups) for t in range(tables)]
    scale = 1.0 / width
    for a in range(len(every)):
        for b in range(a, len(every)):
            row = jnp.sum(every[a] * every[b], axis=0, keepdims=True) * scale
            for x, y in {(a, b), (b, a)} if a != b else {(a, b)}:
                gram[x // tables, pl.ds((x % tables) * len(every) + y, 1), :] = row
    sums = []
    for k in range(1, groups):
        peer = lax.rem(grp + k, groups)
        sums.append(
            pltpu.make_async_remote_copy(
                src_ref=gram.at[peer],
                dst_ref=grams.at[k - 1],
                send_sem=gram_send.at[k - 1],
                recv_sem=gram_recv.at[k - 1],
                device_id={"grp": peer},
                device_id_type=MESH,
            )
        )
        sums[-1].start()
    total = gram[grp]
    for k in range(groups - 1):
        sums[k].wait_recv()
        total = total + grams[k]
    inter_ref[...] = total
    for copy in mixes + sums:
        copy.wait_send()


def finish(n, groups, part):
    sections, tables, width, lanes = part.shape
    pairs = tables * tables * groups
    dma = pltpu.SemaphoreType.DMA
    return pl.pallas_call(
        functools.partial(finish_kernel, n, groups),
        out_shape=(
            jax.ShapeDtypeStruct((tables, width, lanes), jnp.float32),
            jax.ShapeDtypeStruct((pairs, lanes), jnp.float32),
        ),
        in_specs=[VMEM],
        out_specs=(VMEM, VMEM),
        scratch_shapes=[
            pltpu.VMEM((sections - 1, tables, width, lanes), jnp.float32),
            pltpu.VMEM((groups, tables, width // groups, lanes), jnp.float32),
            pltpu.VMEM((groups, pairs, lanes), jnp.float32),
            pltpu.VMEM((groups - 1, pairs, lanes), jnp.float32),
            dma((sections - 1, tables, PIECES)),
            dma((sections - 1, tables, PIECES)),
            dma((groups - 1,)),
            dma((groups - 1,)),
            dma((groups - 1,)),
            dma((groups - 1,)),
        ],
        compiler_params=pltpu.CompilerParams(collective_id=1, has_side_effects=True),
        name="finish",
    )(part)


def solution(mesh):
    n, groups = mesh.shape["blk"], mesh.shape["grp"]

    def shards(tables, bag_ids):
        samples, count, bag = bag_ids.shape
        ids = bag_ids.transpose(1, 2, 0).reshape(count * bag, samples)
        ids = gather_ids(n, ids)
        part = pool(bag, ids, tables)
        pooled, inter = finish(n, groups, part)
        pooled = pooled.transpose(2, 0, 1)
        inter = inter.reshape(count, count * groups, samples).transpose(2, 0, 1)
        return pooled, inter

    return jax.shard_map(
        shards,
        mesh=mesh,
        in_specs=(P("grp", "blk", None), P("blk", "grp", None)),
        out_specs=(P("blk", "grp", None), P("blk", "grp", None)),
        check_vma=False,
    )
```

time: 530 us -> 59.4 us (0.11); the launches traced: 522 us -> 59.3 us
  other arithmetic: 459 us -> 0 us
  Pallas kernels: 0 us -> 56.4 us
  starting transfers between devices: 23.2 us -> 0 us
  matrix products: 11.4 us -> 0 us
  waiting for transfers between devices: 8.9 us -> 0 us
  local copies, waits for them, and re-layouts: 10.5 us -> 2.27 us
  blocking collectives: 7.17 us -> 0 us
    unnamed x26 -> x0, other arithmetic: 456 us -> none
    pallas_call x0 -> x3, Pallas kernels: none -> 56.4 us  [the longest x1 31.8 us: finish(): pl.pallas_call(functools.partial(finish_kernel, n, groups), out_shape=(ja...]
    ppermute x14 -> x0, starting transfers between devices: 23.2 us -> none  [from_behind(): return lax.ppermute(value, axis, pairs)]
    dot_general x17 -> x0, matrix products: 11.4 us -> none  [the longest x16 10.2 us: pool_shard(): jnp.dot(counts, table_rows[table_num], precision=lax.Precision.HIGHEST, p...]
    ppermute x14 -> x0, waiting for transfers between devices: 8.9 us -> none  [from_behind(): return lax.ppermute(value, axis, pairs)]
    all_gather x1 -> x0, blocking collectives: 7.17 us -> none  [shards(): gathered = lax.all_gather(pooled, 'grp', axis=1, tiled=True)]
  transfers between devices with their start and end apart: 14 -> 0, of which waited for: 4 -> 0; matrix products, arithmetic and copies ran while one was open for 40% -> 0% of each run, Pallas kernels for 0% -> 0%
where the time goes in v1:
time: 59.4 us; the launch traced here: 59.3 us
  Pallas kernels  56.4 us (95%)
  local copies, waits for them, and re-layouts  2.27 us (4%)
  between operations  0.65 us (1%)
    pallas_call x1, Pallas kernels, finish(): pl.pallas_call(functools.partial(finish_kernel, n, groups), out_shape=(ja...  31.8 us
    pallas_call x1, Pallas kernels, gather_ids(): pl.pallas_call(functools.partial(gather_ids_kernel, n), out_shape=jax.Sha...  14.2 us
    pallas_call x1, Pallas kernels, pool(): pl.pallas_call(functools.partial(pool_kernel, bag), out_shape=jax.ShapeDt...  10.3 us
    unnamed x4, local copies, waits for them, and re-layouts  2.27 us

profile of v1, /device:TPU:0, one launch (start us, length us, event | category | flops | bytes accessed | tf_op | source)
XLA Modules:
  0.0 59.3 jit_solution(14953318367852587884)
XLA Ops:
  0.6 14.2 %gather_ids.1.ids_ref = s32[512,128]{1,0:T(8,128)} custom-call(s32[64,128]{1,0:T(8,128)} %bitcast.8), custom_call_target="tpu_custom_call" | custom-call | tf_op jit(solution)/shard_map/gather_ids/pallas_call | solution.py:48
  14.9 10.3 %pool.1.part_ref = f32[8,2,128,128]{3,2,1,0:T(8,128)} custom-call(s32[512,128]{1,0:T(8,128)} %gather_ids.1.ids_ref, f32[2,1024,128]{2,1,0:T(8,128)} %table_ref.1), custom_call_target="tpu_custom_call" | custom-call | tf_op jit(solution)/shard_map/pool/pallas_call | solution.py:140
  25.2 31.8 %finish.1 = (f32[2,128,128]{2,1,0:T(8,128)}, f32[16,128]{1,0:T(8,128)}) custom-call(f32[8,2,128,128]{3,2,1,0:T(8,128)} %pool.1.part_ref), custom_call_target="tpu_custom_call" | custom-call | tf_op jit(solution)/shard_map/finish/pallas_call | solution.py:270
  57.1 0.0 copy-start
  57.1 1.7 %copy.4 = f32[128,2,128]{2,1,0:T(2,128)} copy(f32[128,2,128]{0,2,1:T(8,128)} %bitcast.7) | data formatting | bytes 262144
  58.7 0.0 copy-done
  58.7 0.6 %copy.6 = f32[128,2,8]{0,2,1:T(8,128)} copy(f32[128,2,8]{0,2,1:T(8,128)S(1)} %bitcast.9) | data formatting | bytes 16384
Async XLA Ops:
  57.1 1.7 %copy-start = (f32[16,128]{1,0:T(8,128)S(1)}, f32[16,128]{1,0:T(8,128)}, u32[]{:S(2)}) copy-start(f32[16,128]{1,0:T(8,128)} %get-tuple-element.5) | copy-start | bytes 24580

commit v2 on v0

v2 whole, which is shorter than its diff:
```python
import functools

import jax
import jax.numpy as jnp
from jax import lax
from jax.experimental import pallas as pl
from jax.experimental.pallas import tpu as pltpu
from jax.sharding import PartitionSpec as P

SECTIONS = 8
MESH = pl.DeviceIdType.MESH
VMEM = pl.BlockSpec(memory_space=pltpu.VMEM)
CHUNK = 256


def plan(n, tables):
    if n == SECTIONS:
        far, near = n // 2, n - 1 - n // 2
        chains = {}
        for t in range(tables):
            chains[t, 1] = far if t % 2 == 0 else near
            chains[t, -1] = near if t % 2 == 0 else far
        offsets = [far]
        for k in range(near, 0, -1):
            offsets += [k, -k]
        return chains, offsets + [0]
    chains = {(t, 1): SECTIONS - 1 for t in range(tables)}
    return chains, list(range(SECTIONS - 1, -1, -1))


def kernel(n, groups, bag, ids_ref, table_ref, pooled_ref, inter_ref, *scratch):
    near_ids, table_t, keys, counts, sums, held, mixed, gram, grams, *sems = scratch
    ids_send, ids_recv, ring_send, ring_recv, mix_send, mix_recv, gram_send, gram_recv = sems
    tables, rows, width = table_ref.shape
    lanes = ids_ref.shape[1]
    chunks = rows // CHUNK
    quarter = width // groups
    me, grp = lax.axis_index("blk"), lax.axis_index("grp")
    chains, offsets = plan(n, tables)
    order = list(chains)

    if n == SECTIONS:
        place = jnp.where(me % 2 == 0, me // 2, n - 1 - me // 2)
    else:
        place = me

    def at(offset):
        position = lax.rem(place + offset + n, n)
        if n == SECTIONS:
            return jnp.where(position < n // 2, 2 * position, 2 * (n - 1 - position) + 1)
        return position

    barrier = pltpu.get_barrier_semaphore()
    greeted = 0
    for offset in offsets[:-1]:
        pl.semaphore_signal(barrier, inc=1, device_id={"blk": at(offset)}, device_id_type=MESH)
        greeted += 1
        if n != SECTIONS:
            pl.semaphore_signal(barrier, inc=1, device_id={"blk": at(-offset)}, device_id_type=MESH)
            greeted += 1
    for k in range(1, groups):
        pl.semaphore_signal(barrier, inc=1, device_id={"grp": lax.rem(grp + k, groups)}, device_id_type=MESH)
    pl.semaphore_wait(barrier, greeted + groups - 1)

    asks = []
    for job, offset in enumerate(offsets[:-1]):
        asks.append(
            pltpu.make_async_remote_copy(
                src_ref=ids_ref,
                dst_ref=near_ids.at[job],
                send_sem=ids_send.at[job],
                recv_sem=ids_recv.at[job],
                device_id={"blk": at(-offset)},
                device_id_type=MESH,
            )
        )
        asks[-1].start()

    for t in range(tables):
        flipped = table_ref[t].T
        high = flipped.astype(jnp.bfloat16)
        table_t[t, pl.ds(0, width), :] = high
        table_t[t, pl.ds(width, width), :] = (flipped - high.astype(jnp.float32)).astype(jnp.bfloat16)
    index = lax.broadcasted_iota(jnp.int32, (CHUNK, lanes), 0).astype(jnp.float32).astype(jnp.bfloat16)
    one, zero = jnp.bfloat16(1), jnp.bfloat16(0)

    def partial_sums(codes, section):
        local = jnp.where((codes & (SECTIONS - 1)) == section, codes >> 3, -1)
        for c in range(chunks):
            inside = (local >= c * CHUNK) & (local < (c + 1) * CHUNK)
            keys[c] = jnp.where(inside, local - c * CHUNK, 2 * CHUNK).astype(jnp.float32)

        def unit(u, carry):
            t, c = u // chunks, u % chunks
            total = jnp.zeros((CHUNK, lanes), jnp.bfloat16)
            for p in range(bag):
                key = jnp.broadcast_to(keys[c, pl.ds(t * bag + p, 1), :], (CHUNK, lanes))
                total = total + jnp.where(index == key.astype(jnp.bfloat16), one, zero)
            counts[t, pl.ds(pl.multiple_of(c * CHUNK, CHUNK), CHUNK), :] = total
            return carry

        lax.fori_loop(0, tables * chunks, unit, 0)
        result = []
        for t in range(tables):
            both = jnp.dot(table_t[t], counts[t], preferred_element_type=jnp.float32)
            result.append(both[:width] + both[width:])
        return result

    flying = {}
    for job, offset in enumerate(offsets):
        if offset == 0:
            codes = ids_ref[...]
        else:
            asks[job].wait_recv()
            codes = near_ids[job]
        mine = partial_sums(codes, lax.rem(at(offset) + n - me, n))
        for t, way in order:
            slot, hops = order.index((t, way)), chains[t, way]
            away = hops - offset * way % n
            if offset == 0 or away < 0:
                continue
            total = mine[t]
            if away > 0:
                flying[slot, away - 1].wait_recv()
                total = total + held[slot, away - 1]
            sums[slot, away] = total
            flying[slot, away] = pltpu.make_async_remote_copy(
                src_ref=sums.at[slot, away],
                dst_ref=held.at[slot, away],
                send_sem=ring_send.at[slot, away],
                recv_sem=ring_recv.at[slot, away],
                device_id={"blk": at(way)},
                device_id_type=MESH,
            )
            flying[slot, away].start()
    for t, way in order:
        slot, hops = order.index((t, way)), chains[t, way]
        flying[slot, hops - 1].wait_recv()
        mine[t] = mine[t] + held[slot, hops - 1]
    for t in range(tables):
        pooled_ref[t] = mine[t]

    mixes = []
    for k in range(1, groups):
        peer = lax.rem(grp + k, groups)
        mixes.append(
            pltpu.make_async_remote_copy(
                src_ref=pooled_ref.at[:, pl.ds(pl.multiple_of(peer * quarter, quarter), quarter)],
                dst_ref=mixed.at[grp],
                send_sem=mix_send.at[k - 1],
                recv_sem=mix_recv.at[k - 1],
                device_id={"grp": peer},
                device_id_type=MESH,
            )
        )
        mixes[-1].start()
    mixed[grp] = pooled_ref[:, pl.ds(pl.multiple_of(grp * quarter, quarter), quarter)]
    for copy in list(flying.values()) + asks:
        copy.wait_send()
    for copy in mixes:
        copy.wait_recv()
    every = [mixed[g, t] for g in range(groups) for t in range(tables)]
    for a in range(len(every)):
        for b in range(a, len(every)):
            row = jnp.sum(every[a] * every[b], axis=0, keepdims=True) / width
            gram[a // tables, pl.ds((a % tables) * len(every) + b, 1), :] = row
            if a != b:
                gram[b // tables, pl.ds((b % tables) * len(every) + a, 1), :] = row
    parts = []
    for k in range(1, groups):
        peer = lax.rem(grp + k, groups)
        parts.append(
            pltpu.make_async_remote_copy(
                src_ref=gram.at[peer],
                dst_ref=grams.at[k - 1],
                send_sem=gram_send.at[k - 1],
                recv_sem=gram_recv.at[k - 1],
                device_id={"grp": peer},
                device_id_type=MESH,
            )
        )
        parts[-1].start()
    total = gram[grp]
    for k in range(groups - 1):
        parts[k].wait_recv()
        total = total + grams[k]
    inter_ref[...] = total
    for copy in mixes + parts:
        copy.wait_send()


def lookup(n, groups, bag, ids, tables):
    count, rows, width = tables.shape
    lanes = ids.shape[1]
    pairs = count * count * groups
    chains, offsets = plan(n, count)
    hops = max(chains.values())
    dma = pltpu.SemaphoreType.DMA
    ahead = len(offsets) - 1
    return pl.pallas_call(
        functools.partial(kernel, n, groups, bag),
        out_shape=(
            jax.ShapeDtypeStruct((count, width, lanes), jnp.float32),
            jax.ShapeDtypeStruct((pairs, lanes), jnp.float32),
        ),
        in_specs=[VMEM, VMEM],
        out_specs=(VMEM, VMEM),
        scratch_shapes=[
            pltpu.VMEM((ahead, count * bag, lanes), jnp.int32),
            pltpu.VMEM((count, 2 * width, rows), jnp.bfloat16),
            pltpu.VMEM((rows // CHUNK, count * bag, lanes), jnp.float32),
            pltpu.VMEM((count, rows, lanes), jnp.bfloat16),
            pltpu.VMEM((len(chains), hops, width, lanes), jnp.float32),
            pltpu.VMEM((len(chains), hops, width, lanes), jnp.float32),
            pltpu.VMEM((groups, count, width // groups, lanes), jnp.float32),
            pltpu.VMEM((groups, pairs, lanes), jnp.float32),
            pltpu.VMEM((groups - 1, pairs, lanes), jnp.float32),
            dma((ahead,)),
            dma((ahead,)),
            dma((len(chains), hops)),
            dma((len(chains), hops)),
            dma((groups - 1,)),
            dma((groups - 1,)),
            dma((groups - 1,)),
            dma((groups - 1,)),
        ],
        compiler_params=pltpu.CompilerParams(collective_id=0, has_side_effects=True),
        name="lookup",
    )(ids, tables)


def solution(mesh):
    n, groups = mesh.shape["blk"], mesh.shape["grp"]

    def shards(tables, bag_ids):
        samples, count, bag = bag_ids.shape
        ids = bag_ids.transpose(1, 2, 0).reshape(count * bag, samples)
        pooled, inter = lookup(n, groups, bag, ids, tables)
        pooled = pooled.transpose(2, 0, 1)
        inter = inter.reshape(count, count * groups, samples).transpose(2, 0, 1)
        return pooled, inter

    return jax.shard_map(
        shards,
        mesh=mesh,
        in_specs=(P("grp", "blk", None), P("blk", "grp", None)),
        out_specs=(P("blk", "grp", None), P("blk", "grp", None)),
        check_vma=False,
    )
```

time: 530 us -> 43.4 us (0.08); the launches traced: 522 us -> 43.2 us
  other arithmetic: 459 us -> 0 us
  Pallas kernels: 0 us -> 40.3 us
  starting transfers between devices: 23.2 us -> 0 us
  matrix products: 11.4 us -> 0 us
  waiting for transfers between devices: 8.9 us -> 0 us
  local copies, waits for them, and re-layouts: 10.5 us -> 2.27 us
  blocking collectives: 7.17 us -> 0 us
    unnamed x26 -> x0, other arithmetic: 456 us -> none
    pallas_call x0 -> x1, Pallas kernels: none -> 40.3 us  [lookup(): pl.pallas_call(functools.partial(kernel, n, groups, bag), out_shape=(jax....]
    ppermute x14 -> x0, starting transfers between devices: 23.2 us -> none  [from_behind(): return lax.ppermute(value, axis, pairs)]
    dot_general x17 -> x0, matrix products: 11.4 us -> none  [the longest x16 10.2 us: pool_shard(): jnp.dot(counts, table_rows[table_num], precision=lax.Precision.HIGHEST, p...]
    ppermute x14 -> x0, waiting for transfers between devices: 8.9 us -> none  [from_behind(): return lax.ppermute(value, axis, pairs)]
    all_gather x1 -> x0, blocking collectives: 7.17 us -> none  [shards(): gathered = lax.all_gather(pooled, 'grp', axis=1, tiled=True)]
  transfers between devices with their start and end apart: 14 -> 0, of which waited for: 4 -> 0; matrix products, arithmetic and copies ran while one was open for 40% -> 0% of each run, Pallas kernels for 0% -> 0%
where the time goes in v2:
time: 43.4 us; the launch traced here: 43.2 us
  Pallas kernels  40.3 us (93%)
  local copies, waits for them, and re-layouts  2.27 us (5%)
  between operations  0.65 us (1%)
    pallas_call x1, Pallas kernels, lookup(): pl.pallas_call(functools.partial(kernel, n, groups, bag), out_shape=(jax....  40.3 us
    unnamed x4, local copies, waits for them, and re-layouts  2.27 us

profile of v2, /device:TPU:0, one launch (start us, length us, event | category | flops | bytes accessed | tf_op | source)
XLA Modules:
  0.0 43.2 jit_solution(2646263775949669406)
XLA Ops:
  0.6 40.3 %lookup.1 = (f32[2,128,128]{2,1,0:T(8,128)}, f32[16,128]{1,0:T(8,128)}) custom-call(s32[64,128]{1,0:T(8,128)} %bitcast.8, f32[2,1024,128]{2,1,0:T(8,128)} %table_ref.1), custom_call_target="tpu_custom_call" | custom-call | tf_op jit(solution)/shard_map/lookup/pallas_call | solution.py:200
  41.0 0.0 copy-start
  41.0 1.7 %copy.4 = f32[128,2,128]{2,1,0:T(2,128)} copy(f32[128,2,128]{0,2,1:T(8,128)} %bitcast.7) | data formatting | bytes 262144
  42.6 0.0 copy-done
  42.6 0.6 %copy.6 = f32[128,2,8]{0,2,1:T(8,128)} copy(f32[128,2,8]{0,2,1:T(8,128)S(1)} %bitcast.9) | data formatting | bytes 16384
Async XLA Ops:
  41.0 1.7 %copy-start = (f32[16,128]{1,0:T(8,128)S(1)}, f32[16,128]{1,0:T(8,128)}, u32[]{:S(2)}) copy-start(f32[16,128]{1,0:T(8,128)} %get-tuple-element.5) | copy-start | bytes 24580

commit v3 on v2

--- a/solution.py
+++ b/solution.py
@@ -23,13 +23,25 @@
         offsets = [far]
         for k in range(near, 0, -1):
             offsets += [k, -k]
-        return chains, offsets + [0]
+        return chains, offsets
     chains = {(t, 1): SECTIONS - 1 for t in range(tables)}
-    return chains, list(range(SECTIONS - 1, -1, -1))
+    return chains, list(range(SECTIONS - 1, 0, -1))
+
+
+def jobs_of(chains, offsets, n):
+    jobs = []
+    for job, offset in enumerate(offsets):
+        for slot, ((t, way), hops) in enumerate(chains.items()):
+            hop = hops - offset * way % n
+            if hop >= 0:
+                jobs.append((slot, hop, job, t))
+    hops = list(chains.values())
+    longest = max(hops)
+    return sorted(jobs, key=lambda j: (hops[j[0]] * -1 + j[1], j[1] if j[1] < longest - 2 else -hops[j[0]]))
 
 
 def kernel(n, groups, bag, ids_ref, table_ref, pooled_ref, inter_ref, *scratch):
-    near_ids, table_t, keys, counts, sums, held, mixed, gram, grams, *sems = scratch
+    near_ids, table_v, table_sem, own, table_t, keys, counts, sums, held, mixed, gram, grams, *sems = scratch
     ids_send, ids_recv, ring_send, ring_recv, mix_send, mix_recv, gram_send, gram_recv = sems
     tables, rows, width = table_ref.shape
     lanes = ids_ref.shape[1]
@@ -52,7 +64,7 @@
 
     barrier = pltpu.get_barrier_semaphore()
     greeted = 0
-    for offset in offsets[:-1]:
+    for offset in offsets:
         pl.semaphore_signal(barrier, inc=1, device_id={"blk": at(offset)}, device_id_type=MESH)
         greeted += 1
         if n != SECTIONS:
@@ -60,10 +72,12 @@
             greeted += 1
     for k in range(1, groups):
         pl.semaphore_signal(barrier, inc=1, device_id={"grp": lax.rem(grp + k, groups)}, device_id_type=MESH)
+    fetch = pltpu.make_async_copy(table_ref, table_v, table_sem)
+    fetch.start()
     pl.semaphore_wait(barrier, greeted + groups - 1)
 
     asks = []
-    for job, offset in enumerate(offsets[:-1]):
+    for job, offset in enumerate(offsets):
         asks.append(
             pltpu.make_async_remote_copy(
                 src_ref=ids_ref,
@@ -76,76 +90,69 @@
         )
         asks[-1].start()
 
+    fetch.wait()
     for t in range(tables):
-        flipped = table_ref[t].T
+        flipped = table_v[t].T
         high = flipped.astype(jnp.bfloat16)
         table_t[t, pl.ds(0, width), :] = high
         table_t[t, pl.ds(width, width), :] = (flipped - high.astype(jnp.float32)).astype(jnp.bfloat16)
     index = lax.broadcasted_iota(jnp.int32, (CHUNK, lanes), 0).astype(jnp.float32).astype(jnp.bfloat16)
     one, zero = jnp.bfloat16(1), jnp.bfloat16(0)
 
-    def partial_sums(codes, section):
+    def partial_sum(codes, section, t):
         local = jnp.where((codes & (SECTIONS - 1)) == section, codes >> 3, -1)
         for c in range(chunks):
             inside = (local >= c * CHUNK) & (local < (c + 1) * CHUNK)
             keys[c] = jnp.where(inside, local - c * CHUNK, 2 * CHUNK).astype(jnp.float32)
 
-        def unit(u, carry):
-            t, c = u // chunks, u % chunks
+        def unit(c, carry):
             total = jnp.zeros((CHUNK, lanes), jnp.bfloat16)
             for p in range(bag):
-                key = jnp.broadcast_to(keys[c, pl.ds(t * bag + p, 1), :], (CHUNK, lanes))
+                key = jnp.broadcast_to(keys[c, pl.ds(p, 1), :], (CHUNK, lanes))
                 total = total + jnp.where(index == key.astype(jnp.bfloat16), one, zero)
-            counts[t, pl.ds(pl.multiple_of(c * CHUNK, CHUNK), CHUNK), :] = total
+            counts[pl.ds(pl.multiple_of(c * CHUNK, CHUNK), CHUNK), :] = total
             return carry
 
-        lax.fori_loop(0, tables * chunks, unit, 0)
-        result = []
-        for t in range(tables):
-            both = jnp.dot(table_t[t], counts[t], preferred_element_type=jnp.float32)
-            result.append(both[:width] + both[width:])
-        return result
+        lax.fori_loop(0, chunks, unit, 0, unroll=2 if chunks % 2 == 0 else 1)
+        both = jnp.dot(table_t[t], counts[...], preferred_element_type=jnp.float32)
+        return both[:width] + both[width:]
+
+    for t in range(tables):
+        own[t] = partial_sum(ids_ref[pl.ds(t * bag, bag), :], 0, t)
 
     flying = {}
-    for job, offset in enumerate(offsets):
-        if offset == 0:
-            codes = ids_ref[...]
-        else:
+    arrived = set()
+    for slot, hop, job, t in jobs_of(chains, offsets, n):
+        way = order[slot][1]
+        if job not in arrived:
             asks[job].wait_recv()
-            codes = near_ids[job]
-        mine = partial_sums(codes, lax.rem(at(offset) + n - me, n))
-        for t, way in order:
-            slot, hops = order.index((t, way)), chains[t, way]
-            away = hops - offset * way % n
-            if offset == 0 or away < 0:
-                continue
-            total = mine[t]
-            if away > 0:
-                flying[slot, away - 1].wait_recv()
-                total = total + held[slot, away - 1]
-            sums[slot, away] = total
-            flying[slot, away] = pltpu.make_async_remote_copy(
-                src_ref=sums.at[slot, away],
-                dst_ref=held.at[slot, away],
-                send_sem=ring_send.at[slot, away],
-                recv_sem=ring_recv.at[slot, away],
-                device_id={"blk": at(way)},
-                device_id_type=MESH,
-            )
-            flying[slot, away].start()
-    for t, way in order:
-        slot, hops = order.index((t, way)), chains[t, way]
-        flying[slot, hops - 1].wait_recv()
-        mine[t] = mine[t] + held[slot, hops - 1]
-    for t in range(tables):
-        pooled_ref[t] = mine[t]
+            arrived.add(job)
+        section = lax.rem(at(offsets[job]) + n - me, n)
+        total = partial_sum(near_ids[job, pl.ds(t * bag, bag), :], section, t)
+        if hop > 0:
+            flying[slot, hop - 1].wait_recv()
+            total = total + held[slot, hop - 1]
+        sums[slot, hop] = total
+        flying[slot, hop] = pltpu.make_async_remote_copy(
+            src_ref=sums.at[slot, hop],
+            dst_ref=held.at[slot, hop],
+            send_sem=ring_send.at[slot, hop],
+            recv_sem=ring_recv.at[slot, hop],
+            device_id={"blk": at(way)},
+            device_id_type=MESH,
+        )
+        flying[slot, hop].start()
+    for slot, (t, way) in enumerate(order):
+        last = chains[t, way] - 1
+        flying[slot, last].wait_recv()
+        own[t] = own[t] + held[slot, last]
 
     mixes = []
     for k in range(1, groups):
         peer = lax.rem(grp + k, groups)
         mixes.append(
             pltpu.make_async_remote_copy(
-                src_ref=pooled_ref.at[:, pl.ds(pl.multiple_of(peer * quarter, quarter), quarter)],
+                src_ref=own.at[:, pl.ds(pl.multiple_of(peer * quarter, quarter), quarter)],
                 dst_ref=mixed.at[grp],
                 send_sem=mix_send.at[k - 1],
                 recv_sem=mix_recv.at[k - 1],
@@ -154,7 +161,9 @@
             )
         )
         mixes[-1].start()
-    mixed[grp] = pooled_ref[:, pl.ds(pl.multiple_of(grp * quarter, quarter), quarter)]
+    mixed[grp] = own[:, pl.ds(pl.multiple_of(grp * quarter, quarter), quarter)]
+    for t in range(tables):
+        pooled_ref[pl.ds(t, lanes, stride=tables), :] = own[t].T
     for copy in list(flying.values()) + asks:
         copy.wait_send()
     for copy in mixes:
@@ -196,20 +205,23 @@
     chains, offsets = plan(n, count)
     hops = max(chains.values())
     dma = pltpu.SemaphoreType.DMA
-    ahead = len(offsets) - 1
+    ahead = len(offsets)
     return pl.pallas_call(
         functools.partial(kernel, n, groups, bag),
         out_shape=(
-            jax.ShapeDtypeStruct((count, width, lanes), jnp.float32),
+            jax.ShapeDtypeStruct((lanes * count, width), jnp.float32),
             jax.ShapeDtypeStruct((pairs, lanes), jnp.float32),
         ),
-        in_specs=[VMEM, VMEM],
+        in_specs=[VMEM, pl.BlockSpec(memory_space=pl.ANY)],
         out_specs=(VMEM, VMEM),
         scratch_shapes=[
             pltpu.VMEM((ahead, count * bag, lanes), jnp.int32),
+            pltpu.VMEM((count, rows, width), jnp.float32),
+            pltpu.SemaphoreType.DMA,
+            pltpu.VMEM((count, width, lanes), jnp.float32),
             pltpu.VMEM((count, 2 * width, rows), jnp.bfloat16),
-            pltpu.VMEM((rows // CHUNK, count * bag, lanes), jnp.float32),
-            pltpu.VMEM((count, rows, lanes), jnp.bfloat16),
+            pltpu.VMEM((rows // CHUNK, bag, lanes), jnp.float32),
+            pltpu.VMEM((rows, lanes), jnp.bfloat16),
             pltpu.VMEM((len(chains), hops, width, lanes), jnp.float32),
             pltpu.VMEM((len(chains), hops, width, lanes), jnp.float32),
             pltpu.VMEM((groups, count, width // groups, lanes), jnp.float32),
@@ -236,7 +248,7 @@
         samples, count, bag = bag_ids.shape
         ids = bag_ids.transpose(1, 2, 0).reshape(count * bag, samples)
         pooled, inter = lookup(n, groups, bag, ids, tables)
-        pooled = pooled.transpose(2, 0, 1)
+        pooled = pooled.reshape(samples, count, tables.shape[2])
         inter = inter.reshape(count, count * groups, samples).transpose(2, 0, 1)
         return pooled, inter
 

time: 43.4 us -> 43.3 us (level)
  no operation moved by 1% of the time
where the time goes in v3:
time: 43.3 us; the launch traced here: 43.1 us
  Pallas kernels  40.3 us (93%)
  local copies, waits for them, and re-layouts  2.18 us (5%)
  between operations  0.65 us (2%)
    pallas_call x1, Pallas kernels, lookup(): pl.pallas_call(functools.partial(kernel, n, groups, bag), out_shape=(jax....  40.3 us
    unnamed x4, local copies, waits for them, and re-layouts  2.18 us

profile of v3, /device:TPU:0, one launch (start us, length us, event | category | flops | bytes accessed | tf_op | source)
XLA Modules:
  0.0 43.1 jit_solution(160706215555121672)
XLA Ops:
  0.6 40.3 %lookup.1 = (f32[256,128]{1,0:T(8,128)}, f32[16,128]{1,0:T(8,128)}) custom-call(s32[64,128]{1,0:T(8,128)} %bitcast.8, f32[2,1024,128]{2,1,0:T(8,128)} %table_ref.1), custom_call_target="tpu_custom_call" | custom-call | tf_op jit(solution)/shard_map/lookup/pallas_call | solution.py:209
  40.9 0.0 copy-start
  40.9 1.6 %copy.6 = f32[128,2,128]{2,1,0:T(2,128)} copy(f32[128,2,128]{2,1,0:T(2,128)} %bitcast.7) | data formatting | bytes 262144
  42.5 0.0 copy-done
  42.5 0.6 %copy.7 = f32[128,2,8]{0,2,1:T(8,128)} copy(f32[128,2,8]{0,2,1:T(8,128)S(1)} %bitcast.9) | data formatting | bytes 16384
Async XLA Ops:
  40.9 1.6 %copy-start = (f32[16,128]{1,0:T(8,128)S(1)}, f32[16,128]{1,0:T(8,128)}, u32[]{:S(2)}) copy-start(f32[16,128]{1,0:T(8,128)} %get-tuple-element.5) | copy-start | bytes 24580
